TPU v7x, 32 devices: a whole 2x2x4 slice. The times are simulated.
32 devices in a mesh: dp: 4 (over y, x), mx: 4 (over z), my: 2 (over core).
Axes of the slice: x: 2, y: 2, z: 4, core: 2. Of those that a mesh axis runs over, the one named last changes fastest.
Arguments:
- tokens: bfloat16 [8192, 2048], P(('dp', 'my'), 'mx'), may hold values from -6 to 6
- output_grad: bfloat16 [8192, 2048], P(('dp', 'my'), 'mx'), may hold values from -6 to 6
- picture_starts: int32 [8, 2], P('dp'), may hold values from 0 to 768, as said below
- norm1_gain: float32 [2048], P('mx'), may hold values from 0.5 to 1.5
- query_weight: bfloat16 [2048, 2048], P('mx', 'my'), may hold values from -0.5 to 0.5
- key_weight: bfloat16 [2048, 512], P('mx', 'my'), may hold values from -0.5 to 0.5
- value_weight: bfloat16 [2048, 512], P('mx', 'my'), may hold values from -0.125 to 0.125
- out_weight: bfloat16 [2048, 2048], P('my', 'mx'), may hold values from -2 to 2
- norm2_gain: float32 [2048], P('mx'), may hold values from 0.5 to 1.5
- gate_weight: bfloat16 [2048, 8192], P('mx', 'my'), may hold values from -0.125 to 0.125
- up_weight: bfloat16 [2048, 8192], P('mx', 'my'), may hold values from -0.125 to 0.125
- down_weight: bfloat16 [8192, 2048], P('my', 'mx'), may hold values from -0.5 to 0.5
Outputs:
- output: bfloat16 [8192, 2048], P(('dp', 'my'), 'mx')
- input_grad: bfloat16 [8192, 2048], P(('dp', 'my'), 'mx')
- grad_norm1: float32 [2048], P('mx')
- grad_query: float32 [2048, 2048], P('mx', 'my')
- grad_key: float32 [2048, 512], P('mx', 'my')
- grad_value: float32 [2048, 512], P('mx', 'my')
- grad_out: float32 [2048, 2048], P('my', 'mx')
- grad_norm2: float32 [2048], P('mx')
- grad_gate: float32 [2048, 8192], P('mx', 'my')
- grad_up: float32 [2048, 8192], P('mx', 'my')
- grad_down: float32 [8192, 2048], P('my', 'mx')
Inputs may be any that keep to these rules, and one draw needn't show every extreme that they name: `picture_starts`: piece p of a sequence starts at a position from p * 512 to (p + 1) * 512 - 256, so the pieces of a sequence never intersect and lie inside it; some sequence has its first piece at position 0 and some sequence has its last piece ending at the sequence's end.
All inputs are finite; a program needn't handle non-finite values.
Results may differ from a plain program's by a relative error of at most 0.02.
Values may be sent and summed in bfloat16 or wider, within the bound.
No kernel may reach another device: no remote copies, remote signals or barrier semaphores. Data moves between devices by JAX's collectives and lax.ppermute only.
A program may use at most 384 MiB of HBM per device.

v0:
```python
import jax
import jax.numpy as jnp
from jax import lax
from jax.sharding import PartitionSpec as P

D = 2048
HEAD = 64
LEN = 1024
PIECE = 256
epsilon = 1e-05
rope_base = 10000000.0
branch_scale = 0.22
score_scale = 0.015625
masked_score = -1e30


def rope_tables(positions, head_width):
    half_width = head_width // 2
    steps_idx = jnp.arange(half_width, dtype=jnp.float32)
    freqs = jnp.exp(-jnp.log(jnp.float32(rope_base)) * 2.0 * steps_idx / head_width)
    angles = positions.astype(jnp.float32)[:, None] * freqs[None, :]
    cosine = jnp.cos(angles)
    sine = jnp.sin(angles)
    return (jnp.concatenate([cosine, cosine], 1), jnp.concatenate([sine, sine], 1))


def rotate_half(values):
    half_width = values.shape[-1] // 2
    return jnp.concatenate([-values[..., half_width:], values[..., :half_width]], -1)


def apply_rope(values, cosine, sine):
    return values * cosine + rotate_half(values) * sine


def rope_back(values, cosine, sine):
    return values * cosine - rotate_half(values) * sine


def product(left, weight, flipped):
    if flipped:
        return lax.dot_general(
            left, weight, (((1,), (1,)), ((), ())), preferred_element_type=jnp.float32
        )
    return jnp.dot(left, weight, preferred_element_type=jnp.float32)


def outer_sum(left, right):
    return lax.dot_general(
        left, right, (((0,), (0,)), ((), ())), preferred_element_type=jnp.float32
    )


def head_scores(query, key_head, allowed_pairs):
    scores = (
        jnp.einsum("qgd,kd->qgk", query, key_head, preferred_element_type=jnp.float32) * score_scale
    )
    return jnp.where(allowed_pairs[:, None, :], scores, masked_score)


def head_forward(query, key_head, value_head, allowed_pairs):
    scores = head_scores(query, key_head, allowed_pairs)
    row_max = jnp.max(scores, axis=-1, keepdims=True)
    shifted = jnp.exp(scores - row_max)
    row_total = jnp.sum(shifted, axis=-1, keepdims=True)
    probs = shifted / row_total
    mixed = jnp.einsum(
        "qgk,kd->qgd", probs.astype(jnp.bfloat16), value_head, preferred_element_type=jnp.float32
    )
    return (mixed, (row_max + jnp.log(row_total))[..., 0])


def head_backward(query, key_head, value_head, grad_out, log_total, allowed_pairs):
    scores = head_scores(query, key_head, allowed_pairs)
    probs = jnp.exp(scores - log_total[..., None])
    grad_probs = jnp.einsum("qgd,kd->qgk", grad_out, value_head, preferred_element_type=jnp.float32)
    row_dot = jnp.sum(probs * grad_probs, axis=-1, keepdims=True)
    grad_scores = (probs * (grad_probs - row_dot)).astype(jnp.bfloat16)
    grad_query = (
        jnp.einsum("qgk,kd->qgd", grad_scores, key_head, preferred_element_type=jnp.float32)
        * score_scale
    )
    grad_key = (
        jnp.einsum("qgk,qgd->kd", grad_scores, query, preferred_element_type=jnp.float32)
        * score_scale
    )
    grad_value = jnp.einsum(
        "qgk,qgd->kd", probs.astype(jnp.bfloat16), grad_out, preferred_element_type=jnp.float32
    )
    return (grad_query, grad_key, grad_value)


PLANE = ("dp", "my")


def plane_gather(values):
    return lax.all_gather(values, PLANE, axis=0, tiled=True)


def plane_scatter(values):
    return lax.psum_scatter(
        values.astype(jnp.bfloat16), PLANE, scatter_dimension=0, tiled=True
    ).astype(jnp.float32)


def to_rows(values):
    return lax.all_to_all(values, "mx", split_axis=0, concat_axis=1, tiled=True)


def to_tiles(values):
    return lax.all_to_all(values, "mx", split_axis=1, concat_axis=0, tiled=True)


def line_gather(values, axis):
    return lax.all_gather(values, "mx", axis=axis, tiled=True)


def line_scatter(values, axis):
    return lax.psum_scatter(values.astype(jnp.bfloat16), "mx", scatter_dimension=axis, tiled=True)


def norm_forward(stream, gain):
    mean = jnp.mean(stream * stream, axis=1, keepdims=True)
    inverse = lax.rsqrt(mean + epsilon)
    return (inverse, (stream * inverse * gain[None, :]).astype(jnp.bfloat16))


def norm_backward(stream, inverse, gain, grad_normed):
    scaled = gain[None, :] * grad_normed
    row_mean = jnp.mean(stream * scaled, axis=1, keepdims=True)
    grad_stream = inverse * scaled - stream * inverse * inverse * inverse * row_mean
    grad_gain = jnp.sum(grad_normed * stream * inverse, axis=0)
    return (grad_stream, grad_gain)


def piece_of(position, begins):
    inside = (position >= begins) & (position < begins + PIECE)
    number = jnp.arange(1, begins.shape[-1] + 1, dtype=jnp.int32)
    return jnp.sum(jnp.where(inside, number, 0), axis=-1)


def shards(
    tokens,
    output_grad,
    picture_starts,
    norm1_gain,
    query_weight,
    key_weight,
    value_weight,
    out_weight,
    norm2_gain,
    gate_weight,
    up_weight,
    down_weight,
):
    mx_count = lax.axis_size("mx")
    dp_count = lax.axis_size("dp")
    dp_index = lax.axis_index("dp")
    mx_index = lax.axis_index("mx")
    chunk = LEN // mx_count
    seqs = dp_count * lax.axis_size("my")
    rows = seqs * chunk
    query_cols = query_weight.shape[1] // dp_count
    query_heads = query_cols // HEAD
    key_heads = key_weight.shape[1] // HEAD
    share = max(1, dp_count // key_heads)
    key_cols = key_weight.shape[1] * share // dp_count
    own_keys = key_cols // HEAD
    kv_group = query_heads // own_keys
    hidden = gate_weight.shape[1] // dp_count

    def cols(weight, width, index):
        return lax.dynamic_slice_in_dim(weight, index * width, width, axis=1)

    def rows_of(weight, width):
        return lax.dynamic_slice_in_dim(weight, dp_index * width, width, axis=0)

    key_index = dp_index // share
    attn_in = line_gather(
        jnp.concatenate(
            [
                cols(query_weight, query_cols, dp_index),
                cols(key_weight, key_cols, key_index),
                cols(value_weight, key_cols, key_index),
            ],
            axis=1,
        ),
        0,
    )
    attn_back = line_gather(rows_of(out_weight, query_cols), 1)
    ffn_in = line_gather(
        jnp.concatenate(
            [cols(gate_weight, hidden, dp_index), cols(up_weight, hidden, dp_index)], axis=1
        ),
        0,
    )
    ffn_back = line_gather(rows_of(down_weight, hidden), 1)
    gains = line_gather(jnp.stack([norm1_gain, norm2_gain]), 1)
    gain_one, gain_two = (gains[0], gains[1])
    starts = lax.all_gather(picture_starts, "dp", axis=0, tiled=True)
    stream = to_rows(tokens).astype(jnp.float32)
    grad_two = to_rows(output_grad).astype(jnp.float32)
    inverse_one, normed_one = norm_forward(stream, gain_one)
    normed_one_all = plane_gather(normed_one)
    projected = product(normed_one_all, attn_in, False)
    query_pos = mx_index * chunk + jnp.arange(chunk, dtype=jnp.int32)
    key_pos = jnp.arange(LEN, dtype=jnp.int32)
    cosine, sine = rope_tables(query_pos, HEAD)
    cosine = cosine[None, :, None, :]
    sine = sine[None, :, None, :]
    query_piece = piece_of(query_pos[None, :, None], starts[:, None, :])
    key_piece = piece_of(key_pos[None, :, None], starts[:, None, :])
    before = key_pos[None, None, :] <= query_pos[None, :, None]
    same = (query_piece[:, :, None] > 0) & (query_piece[:, :, None] == key_piece[:, None, :])
    allowed_pairs = before | same
    query_rot = apply_rope(
        projected[:, :query_cols].reshape(seqs, chunk, query_heads, HEAD), cosine, sine
    ).astype(jnp.bfloat16)
    key_rot = apply_rope(
        projected[:, query_cols : query_cols + key_cols].reshape(seqs, chunk, own_keys, HEAD),
        cosine,
        sine,
    ).astype(jnp.bfloat16)
    value_own = projected[:, query_cols + key_cols :].astype(jnp.bfloat16)
    key_local = jnp.concatenate(
        [key_rot.reshape(seqs, chunk, key_cols), value_own.reshape(seqs, chunk, key_cols)], axis=2
    )
    key_all = line_gather(key_local, 1)
    query_split = query_rot.reshape(seqs, chunk, own_keys, kv_group, HEAD)
    query_split = query_split.transpose(0, 2, 1, 3, 4).reshape(-1, chunk, kv_group, HEAD)

    def split_keys(values):
        values = values.reshape(seqs, LEN, own_keys, HEAD)
        return values.transpose(0, 2, 1, 3).reshape(-1, LEN, HEAD)

    key_split = split_keys(key_all[:, :, :key_cols])
    value_split = split_keys(key_all[:, :, key_cols:])
    pairs = jnp.repeat(allowed_pairs, own_keys, axis=0)
    mixed, log_totals = lax.map(
        lambda p: head_forward(p[0], p[1], p[2], p[3]), (query_split, key_split, value_split, pairs)
    )

    def join_heads(values):
        values = values.reshape(seqs, own_keys, chunk, kv_group, HEAD).transpose(0, 2, 1, 3, 4)
        return values.reshape(rows, query_cols)

    def split_heads(values):
        values = values.reshape(seqs, chunk, own_keys, kv_group, HEAD).transpose(0, 2, 1, 3, 4)
        return values.reshape(-1, chunk, kv_group, HEAD)

    attn_out = join_heads(mixed).astype(jnp.bfloat16)
    hidden_one = stream + branch_scale * plane_scatter(product(attn_out, attn_back, False))
    inverse_two, normed_two = norm_forward(hidden_one, gain_two)
    normed_two_all = plane_gather(normed_two)
    gate_up = product(normed_two_all, ffn_in, False)
    gate_val = gate_up[:, :hidden]
    up_val = gate_up[:, hidden:]
    sigma = jax.nn.sigmoid(gate_val)
    silu_gate = gate_val * sigma
    hidden_units = (silu_gate * up_val).astype(jnp.bfloat16)
    hidden_two = hidden_one + branch_scale * plane_scatter(product(hidden_units, ffn_back, False))
    output = to_tiles(hidden_two.astype(jnp.bfloat16))
    branch_two = (branch_scale * grad_two).astype(jnp.bfloat16)
    branch_two_all = plane_gather(branch_two)
    grad_down = outer_sum(hidden_units, branch_two_all)
    grad_hidden = product(branch_two_all, ffn_back, True)
    grad_gate_val = (grad_hidden * up_val * sigma * (1.0 + gate_val * (1.0 - sigma))).astype(
        jnp.bfloat16
    )
    grad_up_val = (grad_hidden * silu_gate).astype(jnp.bfloat16)
    grad_gate_up = jnp.concatenate([grad_gate_val, grad_up_val], axis=1)
    grad_ffn_in = outer_sum(normed_two_all, grad_gate_up)
    grad_normed_two = plane_scatter(product(grad_gate_up, ffn_in, True))
    grad_stream_two, grad_norm2 = norm_backward(hidden_one, inverse_two, gain_two, grad_normed_two)
    grad_one = grad_two + grad_stream_two
    branch_one_all = plane_gather((branch_scale * grad_one).astype(jnp.bfloat16))
    grad_out = outer_sum(attn_out, branch_one_all)
    grad_attn = split_heads(product(branch_one_all, attn_back, True).astype(jnp.bfloat16))
    grad_q, grad_k, grad_v = lax.map(
        lambda p: head_backward(p[0], p[1], p[2], p[3], p[4], p[5]),
        (query_split, key_split, value_split, grad_attn, log_totals, pairs),
    )

    def join_keys(values):
        values = values.reshape(seqs, own_keys, LEN, HEAD).transpose(0, 2, 1, 3)
        return values.reshape(seqs, LEN, key_cols)

    key_terms = jnp.concatenate([join_keys(grad_k), join_keys(grad_v)], axis=2)
    key_owned = line_scatter(key_terms, 1).astype(jnp.float32)
    grad_q_pre = rope_back(join_heads(grad_q).reshape(seqs, chunk, query_heads, HEAD), cosine, sine)
    grad_k_pre = rope_back(
        key_owned[:, :, :key_cols].reshape(seqs, chunk, own_keys, HEAD), cosine, sine
    )
    grad_projected = jnp.concatenate(
        [
            grad_q_pre.reshape(rows, query_cols),
            grad_k_pre.reshape(rows, key_cols),
            key_owned[:, :, key_cols:].reshape(rows, key_cols),
        ],
        axis=1,
    ).astype(jnp.bfloat16)
    grad_attn_in = outer_sum(normed_one_all, grad_projected)
    grad_normed_one = plane_scatter(product(grad_projected, attn_in, True))
    grad_stream_one, grad_norm1 = norm_backward(stream, inverse_one, gain_one, grad_normed_one)
    input_grad = to_tiles((grad_one + grad_stream_one).astype(jnp.bfloat16))

    def spread_cols(own):
        return lax.all_gather(own, "dp", axis=1, tiled=True).astype(jnp.float32)

    def spread_rows(own):
        return lax.all_gather(own, "dp", axis=0, tiled=True).astype(jnp.float32)

    def spread_keys(own):
        every = lax.all_gather(own, "dp", axis=0).astype(jnp.float32)
        every = every.reshape(dp_count // share, share, -1, key_cols).sum(axis=1)
        return every.transpose(1, 0, 2).reshape(every.shape[1], -1)

    grad_down = spread_rows(line_scatter(grad_down, 1))
    own_ffn = line_scatter(grad_ffn_in, 0)
    grad_gate = spread_cols(own_ffn[:, :hidden])
    grad_up = spread_cols(own_ffn[:, hidden:])
    grad_out = spread_rows(line_scatter(grad_out, 1))
    own_attn = line_scatter(grad_attn_in, 0)
    grad_query = spread_cols(own_attn[:, :query_cols])
    grad_key = spread_keys(own_attn[:, query_cols : query_cols + key_cols])
    grad_value = spread_keys(own_attn[:, query_cols + key_cols :])
    norms = lax.psum(jnp.stack([grad_norm1, grad_norm2]), ("dp", "mx", "my"))
    norms = lax.dynamic_slice_in_dim(norms, mx_index * norm1_gain.shape[0], norm1_gain.shape[0], 1)
    return (
        output,
        input_grad,
        norms[0],
        grad_query,
        grad_key,
        grad_value,
        grad_out,
        norms[1],
        grad_gate,
        grad_up,
        grad_down,
    )


def solution(mesh):
    placed = (
        P(("dp", "my"), "mx"),
        P(("dp", "my"), "mx"),
        P("dp", None),
        P("mx"),
        P("mx", "my"),
        P("mx", "my"),
        P("mx", "my"),
        P("my", "mx"),
        P("mx"),
        P("mx", "my"),
        P("mx", "my"),
        P("my", "mx"),
    )
    return jax.shard_map(
        shards,
        mesh=mesh,
        in_specs=placed,
        out_specs=(
            P(("dp", "my"), "mx"),
            P(("dp", "my"), "mx"),
            P("mx"),
            P("mx", "my"),
            P("mx", "my"),
            P("mx", "my"),
            P("my", "mx"),
            P("mx"),
            P("mx", "my"),
            P("mx", "my"),
            P("my", "mx"),
        ),
        check_vma=False,
    )
```

profile of v0, /device:TPU:0, one launch (start us, length us, event | category | flops | bytes accessed | tf_op | source)
XLA Modules:
  0.0 1764.2 jit_solution(13706677136220090018)
XLA Ops:
  15.8 45.3 %all_gather.61 = f32[2,2048]{1,0:T(2,128)S(1)} all-gather(f32[2,512]{1,0:T(2,128)S(1)} %pad_maximum_fusion.10), channel_id=1, replica_groups=mesh['dp'=4,'mx'=4,'my'=2] {'mx'}, dimensions={1}, use_global_device_ids=true | all-gather | bytes 20480 | tf_op jit(solution)/shard_map/all_gather | solution.py:115
  65.7 55.6 %all-gather.18.cloned.1.call-done = bf16[2048,2048]{1,0:T(8,128)(2,1)} async-done(((bf16[256,2048]{1,0:T(8,128)(2,1)}), bf16[2048,2048]{1,0:T(8,128)(2,1)}) %all-gather.18.cloned.1.call-update) | async-done | bytes 8388624 | tf_op jit(solution)/shard_map/all_gather | solution.py:97
  148.5 28.1 %all-gather.22.cloned.1.call-done = bf16[8,1024,128]{1,2,0:T(8,128)(2,1)} async-done(((bf16[8,256,128]{1,2,0:T(8,128)(2,1)}), bf16[8,1024,128]{1,2,0:T(8,128)(2,1)}) %all-gather.22.cloned.1.call-update) | async-done | bytes 2097168 | tf_op jit(solution)/shard_map/all_gather | solution.py:115
  179.7 57.7 %while.28 = (s32[]{:T(128)}, bf16[8,256,4,64]{1,3,2,0:T(8,128)(2,1)}, f32[8,256,4]{1,2,0:T(4,128)S(1)}, pred[8,256,1024]{2,1,0:T(8,128)(4,1)}, bf16[8,256,4,64]{...) while((s32[]{:T(128)}, bf16[8,256,4,64]{1,3,2,0:T(8,128)(2,1)}, ...), condition=%wide.region_6.7_spmd.clone, body=%wide.region_3.6_spmd.sunk.clone | while | flops 281017344 | bytes 14583893 | solution.py:239
  250.4 66.5 %reduce-scatter.10.cloned.1.call-done = bf16[256,2048]{1,0:T(8,128)(2,1)} async-done(((bf16[2048,2048]{1,0:T(8,128)(2,1)}), bf16[256,2048]{1,0:T(8,128)(2,1)}) %reduce-scatter.10.cloned.1.call-update) | async-done | bytes 1048592 | tf_op jit(solution)/shard_map/reduce_scatter | solution.py:101
  322.5 57.9 %all_to_all.64 = bf16[4,256,512]{2,1,0:T(8,128)(2,1)S(1)} all-to-all(bf16[4,256,512]{2,1,0:T(8,128)(2,1)} %bitcast.282), channel_id=1, replica_groups=mesh['dp'=4,'mx'=4,'my'=2] {'mx'}, dimensions={0} | all-to-all | bytes 2097152 | tf_op jit(solution)/shard_map/all_to_all | solution.py:107
  383.7 104.4 %all-gather.28.cloned.1.call-done = bf16[2048,2048]{1,0:T(8,128)(2,1)} async-done(((bf16[512,2048]{1,0:T(8,128)(2,1)}), bf16[2048,2048]{1,0:T(8,128)(2,1)}) %all-gather.28.cloned.1.call-update) | async-done | bytes 8388624 | tf_op jit(solution)/shard_map/all_gather | solution.py:115
  488.1 54.9 %all-gather.26.cloned.1.call-done = bf16[2048,2048]{1,0:T(8,128)(2,1)} async-done(((bf16[256,2048]{1,0:T(8,128)(2,1)}), bf16[2048,2048]{1,0:T(8,128)(2,1)}) %all-gather.26.cloned.1.call-update) | async-done | bytes 8388624 | tf_op jit(solution)/shard_map/all_gather | solution.py:97
  543.0 24.3 %fusion.93 = f32[2048,2048]{0,1:T(8,128)} fusion(bf16[2048,2048]{1,0:T(8,128)(2,1)} %all-gather.26.cloned.1.call-done, bf16[2048,2048]{1,0:T(8,128)(2,1)} %all-gather.28.cloned.1.call-done), kind=kOutput, calls=%fused_computation.183 | convolution fusion | flops 17179869184 | bytes 33554432 | tf_op jit(solution)/shard_map/dot_general | solution.py:45
  567.3 58.6 %all-gather.30.cloned.1.call-done = bf16[1024,2048]{1,0:T(8,128)(2,1)} async-done(((bf16[1024,512]{1,0:T(8,128)(2,1)}), bf16[1024,2048]{1,0:T(8,128)(2,1)}) %all-gather.30.cloned.1.call-update) | async-done | bytes 4194320 | tf_op jit(solution)/shard_map/all_gather | solution.py:115
  625.9 55.2 %all-gather.32.cloned.1.call-done = bf16[2048,2048]{1,0:T(8,128)(2,1)} async-done(((bf16[256,2048]{1,0:T(8,128)(2,1)}), bf16[2048,2048]{1,0:T(8,128)(2,1)}) %all-gather.32.cloned.1.call-update) | async-done | bytes 8388624 | tf_op jit(solution)/shard_map/all_gather | solution.py:97
  727.5 71.6 %reduce-scatter.14.cloned.1.call-done = bf16[256,2048]{1,0:T(8,128)(2,1)} async-done(((bf16[2048,2048]{1,0:T(8,128)(2,1)}), bf16[256,2048]{1,0:T(8,128)(2,1)}) %reduce-scatter.14.cloned.1.call-update) | async-done | bytes 1048592 | tf_op jit(solution)/shard_map/reduce_scatter | solution.py:101
  803.9 54.3 %all-gather.34.cloned.1.call-done = bf16[2048,2048]{1,0:T(8,128)(2,1)} async-done(((bf16[256,2048]{1,0:T(8,128)(2,1)}), bf16[2048,2048]{1,0:T(8,128)(2,1)}) %all-gather.34.cloned.1.call-update) | async-done | bytes 8388624 | tf_op jit(solution)/shard_map/all_gather | solution.py:97
  867.5 109.9 %while.29 = (s32[]{:T(128)}, f32[8,256,4,64]{1,3,2,0:T(8,128)}, bf16[8,1024,64]{1,2,0:T(8,128)(2,1)}, bf16[8,1024,64]{1,2,0:T(8,128)(2,1)}, pred[8,256,1024]{2,1...) while((s32[]{:T(128)}, f32[8,256,4,64]{1,3,2,0:T(8,128)}, ...), condition=%wide.region_14.15_spmd.clone, body=%wide.region_12.14_spmd.sunk.clone | while | flops 686947328 | bytes 34505836 | solution.py:279
  1064.5 38.1 %reduce-scatter.26.cloned.1.call-done = bf16[1024,512]{1,0:T(8,128)(2,1)} async-done(((bf16[1024,2048]{1,0:T(8,128)(2,1)}), bf16[1024,512]{1,0:T(8,128)(2,1)}) %reduce-scatter.26.cloned.1.call-update) | async-done | bytes 1048592 | tf_op jit(solution)/shard_map/reduce_scatter | solution.py:119
  1102.6 147.9 %reduce-scatter.24.cloned.1.call-done = bf16[512,2048]{1,0:T(8,128)(2,1)} async-done(((bf16[2048,2048]{1,0:T(8,128)(2,1)}), bf16[512,2048]{1,0:T(8,128)(2,1)}) %reduce-scatter.24.cloned.1.call-update) | async-done | bytes 2097168 | tf_op jit(solution)/shard_map/reduce_scatter | solution.py:119
  1254.3 26.2 %reduce-scatter.22.cloned.1.call-done = bf16[256,512]{1,0:T(8,128)(2,1)} async-done(((bf16[256,2048]{1,0:T(8,128)(2,1)}), bf16[256,512]{1,0:T(8,128)(2,1)}) %reduce-scatter.22.cloned.1.call-update) | async-done | bytes 262160 | tf_op jit(solution)/shard_map/reduce_scatter | solution.py:119
  1280.6 73.9 %reduce-scatter.18.cloned.1.call-done = bf16[256,2048]{1,0:T(8,128)(2,1)} async-done(((bf16[2048,2048]{1,0:T(8,128)(2,1)}), bf16[256,2048]{1,0:T(8,128)(2,1)}) %reduce-scatter.18.cloned.1.call-update) | async-done | bytes 1048592 | tf_op jit(solution)/shard_map/reduce_scatter | solution.py:101
  1356.4 73.5 %reduce-scatter.12.cloned.1.call-done = bf16[256,2048]{1,0:T(8,128)(2,1)} async-done(((bf16[2048,2048]{1,0:T(8,128)(2,1)}), bf16[256,2048]{1,0:T(8,128)(2,1)}) %reduce-scatter.12.cloned.1.call-update) | async-done | bytes 1048592 | tf_op jit(solution)/shard_map/reduce_scatter | solution.py:101
  1440.1 44.9 %reduce-scatter.20.cloned.1.call-done = bf16[512,384]{1,0:T(8,128)(2,1)} async-done(((bf16[2048,384]{1,0:T(8,128)(2,1)}), bf16[512,384]{1,0:T(8,128)(2,1)}) %reduce-scatter.20.cloned.1.call-update) | async-done | bytes 393232 | tf_op jit(solution)/shard_map/reduce_scatter | solution.py:119
  1495.3 47.7 %all-gather.44.cloned.1.call-done = bf16[4096,512]{1,0:T(8,128)(2,1)} async-done(((bf16[1024,512]{1,0:T(8,128)(2,1)}), bf16[4096,512]{1,0:T(8,128)(2,1)}) %all-gather.44.cloned.1.call-update) | async-done | bytes 4194320 | tf_op jit(solution)/shard_map/all_gather | solution.py:311
  1549.7 48.1 %all-gather.40.cloned.1.call-done = bf16[512,4096]{1,0:T(8,128)(2,1)} async-done(((bf16[512,1024]{1,0:T(8,128)(2,1)}), bf16[512,4096]{1,0:T(8,128)(2,1)}) %all-gather.40.cloned.1.call-update) | async-done | bytes 4194320 | tf_op jit(solution)/shard_map/all_gather | solution.py:308
  1604.5 48.4 %all-gather.42.cloned.1.call-done = bf16[512,4096]{1,0:T(8,128)(2,1)} async-done(((bf16[512,1024]{1,0:T(8,128)(2,1)}), bf16[512,4096]{1,0:T(8,128)(2,1)}) %all-gather.42.cloned.1.call-update) | async-done | bytes 4194320 | tf_op jit(solution)/shard_map/all_gather | solution.py:308
  1715.6 38.9 %psum.7 = f32[2,2048]{1,0:T(2,128)S(1)} all-reduce(f32[2,2048]{1,0:T(2,128)S(1)} %pad_maximum_fusion.9), channel_id=1, replica_groups=mesh['dp'=4,'mx'=4,'my'=2] {'dp','mx','my'}, use_global_device_ids=true, to_apply=%region_20.21 | all-reduce | flops 4096 | bytes 32768 | tf_op jit(solution)/shard_map/psum | solution.py:327
  (342 shorter events, 484.4 us)
Async XLA Ops:
  7.2 54.0 %all-to-all-start = ((bf16[4,256,512]{2,1,0:T(8,128)(2,1)}), bf16[4,256,512]{2,1,0:T(8,128)(2,1)S(1)}, u32[]{:S(2)}, u32[]{:S(2)}) async-start(bf16[4,256,512]{2,1,0:T(8,128)(2,1)} %bitcast.281), calls=%async_computation | async-start | bytes 2097152 | tf_op jit(solution)/shard_map/all_to_all | solution.py:107
  15.8 105.5 %all-gather.18.cloned.1.call-start = ((), (), s32[]{:S(2)}) async-start(), calls=%async_computation.13 | async-start | bytes 9437184 | tf_op jit(solution)/shard_map/all_gather | solution.py:97
  65.4 111.2 %all-gather.22.cloned.1.call-start = ((), (), s32[]{:S(2)}) async-start(), calls=%async_computation.15 | async-start | bytes 2621440 | tf_op jit(solution)/shard_map/all_gather | solution.py:115
  130.2 109.4 %all-gather.24.cloned.1.call-start = ((), (), s32[]{:S(2)}) async-start(), calls=%async_computation.16 | async-start | bytes 1310720 | tf_op jit(solution)/shard_map/all_gather | solution.py:115
  131.9 184.9 %reduce-scatter.10.cloned.1.call-start = ((), (), s32[]{:S(2)}) async-start(), calls=%async_computation.17 | async-start | bytes 9437184 | tf_op jit(solution)/shard_map/reduce_scatter | solution.py:101
  247.0 241.1 %all-gather.28.cloned.1.call-start = ((), (), s32[]{:S(2)}) async-start(), calls=%async_computation.19 | async-start | bytes 10485760 | tf_op jit(solution)/shard_map/all_gather | solution.py:115
  250.3 292.7 %all-gather.26.cloned.1.call-start = ((), (), s32[]{:S(2)}) async-start(), calls=%async_computation.18 | async-start | bytes 9437184 | tf_op jit(solution)/shard_map/all_gather | solution.py:97
  320.1 305.8 %all-gather.30.cloned.1.call-start = ((), (), s32[]{:S(2)}) async-start(), calls=%async_computation.20 | async-start | bytes 5242880 | tf_op jit(solution)/shard_map/all_gather | solution.py:115
  322.4 358.7 %all-gather.32.cloned.1.call-start = ((), (), s32[]{:S(2)}) async-start(), calls=%async_computation.22 | async-start | bytes 9437184 | tf_op jit(solution)/shard_map/all_gather | solution.py:97
  383.4 415.7 %reduce-scatter.14.cloned.1.call-start = ((), (), s32[]{:S(2)}) async-start(), calls=%async_computation.23 | async-start | bytes 9437184 | tf_op jit(solution)/shard_map/reduce_scatter | solution.py:101
  727.4 130.8 %all-gather.34.cloned.1.call-start = ((), (), s32[]{:S(2)}) async-start(), calls=%async_computation.24 | async-start | bytes 9437184 | tf_op jit(solution)/shard_map/all_gather | solution.py:97
  803.8 227.6 %reduce-scatter.16.cloned.1.call-start = ((), (), s32[]{:S(2)}) async-start(), calls=%async_computation.25 | async-start | bytes 2621440 | tf_op jit(solution)/shard_map/reduce_scatter | solution.py:119
  980.4 122.1 %reduce-scatter.26.cloned.1.call-start = ((), (), s32[]{:S(2)}) async-start(), calls=%async_computation.34 | async-start | bytes 5242880 | tf_op jit(solution)/shard_map/reduce_scatter | solution.py:119
  994.4 256.1 %reduce-scatter.24.cloned.1.call-start = ((), (), s32[]{:S(2)}) async-start(), calls=%async_computation.31 | async-start | bytes 10485760 | tf_op jit(solution)/shard_map/reduce_scatter | solution.py:119
  1018.4 262.2 %reduce-scatter.22.cloned.1.call-start = ((), (), s32[]{:S(2)}) async-start(), calls=%async_computation.29 | async-start | bytes 1310720 | tf_op jit(solution)/shard_map/reduce_scatter | solution.py:119
  1028.3 326.2 %reduce-scatter.18.cloned.1.call-start = ((), (), s32[]{:S(2)}) async-start(), calls=%async_computation.26 | async-start | bytes 9437184 | tf_op jit(solution)/shard_map/reduce_scatter | solution.py:101
  1040.9 389.0 %reduce-scatter.12.cloned.1.call-start = ((), (), s32[]{:S(2)}) async-start(), calls=%async_computation.21 | async-start | bytes 9437184 | tf_op jit(solution)/shard_map/reduce_scatter | solution.py:101
  1055.2 429.7 %reduce-scatter.20.cloned.1.call-start = ((), (), s32[]{:S(2)}) async-start(), calls=%async_computation.27 | async-start | bytes 1966080 | tf_op jit(solution)/shard_map/reduce_scatter | solution.py:119
  1064.4 478.5 %all-gather.44.cloned.1.call-start = ((), (), s32[]{:S(2)}) async-start(), calls=%async_computation.35 | async-start | bytes 5242880 | tf_op jit(solution)/shard_map/all_gather | solution.py:311
  1102.6 495.2 %all-gather.40.cloned.1.call-start = ((), (), s32[]{:S(2)}) async-start(), calls=%async_computation.32 | async-start | bytes 5242880 | tf_op jit(solution)/shard_map/all_gather | solution.py:308
  1253.6 399.3 %all-gather.42.cloned.1.call-start = ((), (), s32[]{:S(2)}) async-start(), calls=%async_computation.33 | async-start | bytes 5242880 | tf_op jit(solution)/shard_map/all_gather | solution.py:308
  1254.3 426.9 %all-gather.38.cloned.1.call-start = ((), (), s32[]{:S(2)}) async-start(), calls=%async_computation.30 | async-start | bytes 1310720 | tf_op jit(solution)/shard_map/all_gather | solution.py:311
  1440.1 272.8 %all-gather.36.cloned.1.call-start = ((), (), s32[]{:S(2)}) async-start(), calls=%async_computation.28 | async-start | bytes 1310720 | tf_op jit(solution)/shard_map/all_gather | solution.py:308
  1489.2 266.0 %all-to-all-start.3 = ((bf16[256,4,512]{2,0,1:T(8,128)(2,1)}), bf16[256,4,512]{2,0,1:T(8,128)(2,1)S(1)}, u32[]{:S(2)}, u32[]{:S(2)}) async-start(bf16[256,4,512]{2,0,1:T(8,128)(2,1)} %bitcast.272), calls=%async_computation.8 | async-start | bytes 2097152 | tf_op jit(solution)/shard_map/all_to_all | solution.py:111
  (39 other events, 3912.1 us)
Sparse Core Ops, SparseCore 0:
  16.6 48.6 all-gather.19
  67.8 53.4 all-gather.17
  130.3 46.2 all-gather.21
  178.6 26.1 all-gather.23
  247.2 69.6 reduce-scatter.9
  318.9 169.1 all-gather.27
  490.6 52.3 all-gather.25
  545.1 80.7 all-gather.29
  628.4 52.7 all-gather.31
  727.5 71.4 reduce-scatter.13
  803.9 54.2 all-gather.33
  980.6 43.6 reduce-scatter.15
  1026.5 75.9 reduce-scatter.25
  1105.3 145.1 reduce-scatter.23
  1252.6 27.8 reduce-scatter.21
  1284.4 70.0 reduce-scatter.17
  1358.4 71.4 reduce-scatter.11
  1432.6 52.2 reduce-scatter.19
  1486.8 56.1 all-gather.43
  1545.2 52.5 all-gather.39
  1600.3 52.5 all-gather.41
  1654.7 26.4 all-gather.37
  1683.1 28.7 all-gather.35
where the time goes:
time: 1770 us; the launch traced here: 1760 us
  waiting for transfers between devices  1120 us (63%)
  matrix products  297 us (17%)
  blocking collectives  175 us (10%)
  other arithmetic  82.7 us (5%)
  local copies, waits for them, and re-layouts  54.2 us (3%)
  starting transfers between devices  18.3 us (1%)
    reduce_scatter x4, waiting for transfers between devices, plane_scatter(): lax.psum_scatter(values.astype(jnp.bfloat16), PLANE, scatter_dimension=0,...  286 us
    reduce_scatter x5, waiting for transfers between devices, line_scatter(): lax.psum_scatter(values.astype(jnp.bfloat16), 'mx', scatter_dimension=axi...  257 us
    all_gather x4, waiting for transfers between devices, plane_gather(): return lax.all_gather(values, PLANE, axis=0, tiled=True)  220 us
    all_gather x5, waiting for transfers between devices, line_gather(): return lax.all_gather(values, 'mx', axis=axis, tiled=True)  191 us
    all_gather x3, waiting for transfers between devices, spread_cols(): return lax.all_gather(own, 'dp', axis=1, tiled=True).astype(jnp.float32)  96.4 us
    all_gather x2, waiting for transfers between devices, spread_rows(): return lax.all_gather(own, 'dp', axis=0, tiled=True).astype(jnp.float32)  69.4 us
    dot_general x4, matrix products, product(): lax.dot_general(left, weight, (((1,), (1,)), ((), ())), preferred_element...  59.1 us
    all_to_all x1, blocking collectives, to_rows(): return lax.all_to_all(values, 'mx', split_axis=0, concat_axis=1, tiled=True)  57.9 us
  transfers between devices with their start and end apart: 26, of which 20 were waited for; matrix products, arithmetic and copies ran while one was open for 13% of the time, Pallas kernels for 0%

commit v1 on v0

--- a/solution.py
+++ b/solution.py
@@ -104,7 +104,13 @@
 
 
 def to_rows(values):
-    return lax.all_to_all(values, "mx", split_axis=0, concat_axis=1, tiled=True)
+
+    def meet_paths(w_in, across):
+        return jnp.concatenate(
+            lax.all_to_all(jnp.stack(jnp.split(w_in, lax.psum(1, across), 0), 0), across, 0, 0), 1
+        )
+
+    return meet_paths(values, "mx")
 
 
 def to_tiles(values):

time: 1770 us -> 1770 us (level)
  no operation moved by 1% of the time
where the time goes in v1:
time: 1770 us
  waiting for transfers between devices  1120 us (63%)
  matrix products  297 us (17%)
  blocking collectives  176 us (10%)
  other arithmetic  83.9 us (5%)
  local copies, waits for them, and re-layouts  55.9 us (3%)
  starting transfers between devices  17.9 us (1%)
    reduce_scatter x4, waiting for transfers between devices, plane_scatter(): lax.psum_scatter(values.astype(jnp.bfloat16), PLANE, scatter_dimension=0,...  286 us
    reduce_scatter x5, waiting for transfers between devices, line_scatter(): lax.psum_scatter(values.astype(jnp.bfloat16), 'mx', scatter_dimension=axi...  257 us
    all_gather x4, waiting for transfers between devices, plane_gather(): return lax.all_gather(values, PLANE, axis=0, tiled=True)  220 us
    all_gather x5, waiting for transfers between devices, line_gather(): return lax.all_gather(values, 'mx', axis=axis, tiled=True)  191 us
    all_gather x3, waiting for transfers between devices, spread_cols(): return lax.all_gather(own, 'dp', axis=1, tiled=True).astype(jnp.float32)  96.4 us
    all_gather x2, waiting for transfers between devices, spread_rows(): return lax.all_gather(own, 'dp', axis=0, tiled=True).astype(jnp.float32)  69.4 us
    dot_general x4, matrix products, product(): lax.dot_general(left, weight, (((1,), (1,)), ((), ())), preferred_element...  59.2 us
    all_to_all x1, blocking collectives, meet_paths(): lax.all_to_all(jnp.stack(jnp.split(w_in, lax.psum(1, across), 0), 0), acr...  58.3 us
  transfers between devices with their start and end apart: 26, of which 20 were waited for; matrix products, arithmetic and copies ran while one was open for 13% of the time, Pallas kernels for 0%

profile of v1, /device:TPU:0, one launch (start us, length us, event | category | flops | bytes accessed | tf_op | source)
XLA Modules:
  0.0 1768.0 jit_solution(5059973860310798623)
XLA Ops:
  17.3 46.3 %all_gather.61 = f32[2,2048]{1,0:T(2,128)S(1)} all-gather(f32[2,512]{1,0:T(2,128)S(1)} %pad_maximum_fusion.12), channel_id=1, replica_groups=mesh['dp'=4,'mx'=4,'my'=2] {'mx'}, dimensions={1}, use_global_device_ids=true | all-gather | bytes 20480 | tf_op jit(solution)/shard_map/all_gather | solution.py:121
  68.1 55.6 %all-gather.18.cloned.1.call-done = bf16[2048,2048]{1,0:T(8,128)(2,1)} async-done(((bf16[256,2048]{1,0:T(8,128)(2,1)}), bf16[2048,2048]{1,0:T(8,128)(2,1)}) %all-gather.18.cloned.1.call-update) | async-done | bytes 8388624 | tf_op jit(solution)/shard_map/all_gather | solution.py:97
  150.9 28.1 %all-gather.22.cloned.1.call-done = bf16[8,1024,128]{1,2,0:T(8,128)(2,1)} async-done(((bf16[8,256,128]{1,2,0:T(8,128)(2,1)}), bf16[8,1024,128]{1,2,0:T(8,128)(2,1)}) %all-gather.22.cloned.1.call-update) | async-done | bytes 2097168 | tf_op jit(solution)/shard_map/all_gather | solution.py:121
  182.1 57.7 %while.28 = (s32[]{:T(128)}, bf16[8,256,4,64]{1,3,2,0:T(8,128)(2,1)}, f32[8,256,4]{1,2,0:T(4,128)S(1)}, pred[8,256,1024]{2,1,0:T(8,128)(4,1)}, bf16[8,256,4,64]{...) while((s32[]{:T(128)}, bf16[8,256,4,64]{1,3,2,0:T(8,128)(2,1)}, ...), condition=%wide.region_6.7_spmd.clone, body=%wide.region_3.6_spmd.sunk.clone | while | flops 281017344 | bytes 14583893 | solution.py:245
  252.7 66.5 %reduce-scatter.10.cloned.1.call-done = bf16[256,2048]{1,0:T(8,128)(2,1)} async-done(((bf16[2048,2048]{1,0:T(8,128)(2,1)}), bf16[256,2048]{1,0:T(8,128)(2,1)}) %reduce-scatter.10.cloned.1.call-update) | async-done | bytes 1048592 | tf_op jit(solution)/shard_map/reduce_scatter | solution.py:101
  326.3 58.3 %all_to_all.48 = bf16[4,256,512]{2,1,0:T(8,128)(2,1)S(1)} all-to-all(bf16[4,256,512]{2,1,0:T(8,128)(2,1)S(1)} %pad_maximum_fusion.6), channel_id=1, replica_groups=mesh['dp'=4,'mx'=4,'my'=2] {'mx'}, dimensions={0} | all-to-all | bytes 2097152 | tf_op jit(solution)/shard_map/all_to_all | solution.py:110
  387.6 104.3 %all-gather.28.cloned.1.call-done = bf16[2048,2048]{1,0:T(8,128)(2,1)} async-done(((bf16[512,2048]{1,0:T(8,128)(2,1)}), bf16[2048,2048]{1,0:T(8,128)(2,1)}) %all-gather.28.cloned.1.call-update) | async-done | bytes 8388624 | tf_op jit(solution)/shard_map/all_gather | solution.py:121
  491.9 54.9 %all-gather.26.cloned.1.call-done = bf16[2048,2048]{1,0:T(8,128)(2,1)} async-done(((bf16[256,2048]{1,0:T(8,128)(2,1)}), bf16[2048,2048]{1,0:T(8,128)(2,1)}) %all-gather.26.cloned.1.call-update) | async-done | bytes 8388624 | tf_op jit(solution)/shard_map/all_gather | solution.py:97
  546.8 24.3 %fusion.93 = f32[2048,2048]{0,1:T(8,128)} fusion(bf16[2048,2048]{1,0:T(8,128)(2,1)} %all-gather.26.cloned.1.call-done, bf16[2048,2048]{1,0:T(8,128)(2,1)} %all-gather.28.cloned.1.call-done), kind=kOutput, calls=%fused_computation.193 | convolution fusion | flops 17179869184 | bytes 33554432 | tf_op jit(solution)/shard_map/dot_general | solution.py:45
  571.1 58.6 %all-gather.30.cloned.1.call-done = bf16[1024,2048]{1,0:T(8,128)(2,1)} async-done(((bf16[1024,512]{1,0:T(8,128)(2,1)}), bf16[1024,2048]{1,0:T(8,128)(2,1)}) %all-gather.30.cloned.1.call-update) | async-done | bytes 4194320 | tf_op jit(solution)/shard_map/all_gather | solution.py:121
  629.7 55.2 %all-gather.32.cloned.1.call-done = bf16[2048,2048]{1,0:T(8,128)(2,1)} async-done(((bf16[256,2048]{1,0:T(8,128)(2,1)}), bf16[2048,2048]{1,0:T(8,128)(2,1)}) %all-gather.32.cloned.1.call-update) | async-done | bytes 8388624 | tf_op jit(solution)/shard_map/all_gather | solution.py:97
  731.3 71.6 %reduce-scatter.14.cloned.1.call-done = bf16[256,2048]{1,0:T(8,128)(2,1)} async-done(((bf16[2048,2048]{1,0:T(8,128)(2,1)}), bf16[256,2048]{1,0:T(8,128)(2,1)}) %reduce-scatter.14.cloned.1.call-update) | async-done | bytes 1048592 | tf_op jit(solution)/shard_map/reduce_scatter | solution.py:101
  807.7 54.3 %all-gather.34.cloned.1.call-done = bf16[2048,2048]{1,0:T(8,128)(2,1)} async-done(((bf16[256,2048]{1,0:T(8,128)(2,1)}), bf16[2048,2048]{1,0:T(8,128)(2,1)}) %all-gather.34.cloned.1.call-update) | async-done | bytes 8388624 | tf_op jit(solution)/shard_map/all_gather | solution.py:97
  871.3 109.9 %while.29 = (s32[]{:T(128)}, f32[8,256,4,64]{1,3,2,0:T(8,128)}, bf16[8,1024,64]{1,2,0:T(8,128)(2,1)}, bf16[8,1024,64]{1,2,0:T(8,128)(2,1)}, pred[8,256,1024]{2,1...) while((s32[]{:T(128)}, f32[8,256,4,64]{1,3,2,0:T(8,128)}, ...), condition=%wide.region_14.15_spmd.clone, body=%wide.region_12.14_spmd.sunk.clone | while | flops 686947328 | bytes 34505836 | solution.py:285
  1068.3 38.0 %reduce-scatter.26.cloned.1.call-done = bf16[1024,512]{1,0:T(8,128)(2,1)} async-done(((bf16[1024,2048]{1,0:T(8,128)(2,1)}), bf16[1024,512]{1,0:T(8,128)(2,1)}) %reduce-scatter.26.cloned.1.call-update) | async-done | bytes 1048592 | tf_op jit(solution)/shard_map/reduce_scatter | solution.py:125
  1106.5 147.9 %reduce-scatter.24.cloned.1.call-done = bf16[512,2048]{1,0:T(8,128)(2,1)} async-done(((bf16[2048,2048]{1,0:T(8,128)(2,1)}), bf16[512,2048]{1,0:T(8,128)(2,1)}) %reduce-scatter.24.cloned.1.call-update) | async-done | bytes 2097168 | tf_op jit(solution)/shard_map/reduce_scatter | solution.py:125
  1258.2 26.2 %reduce-scatter.22.cloned.1.call-done = bf16[256,512]{1,0:T(8,128)(2,1)} async-done(((bf16[256,2048]{1,0:T(8,128)(2,1)}), bf16[256,512]{1,0:T(8,128)(2,1)}) %reduce-scatter.22.cloned.1.call-update) | async-done | bytes 262160 | tf_op jit(solution)/shard_map/reduce_scatter | solution.py:125
  1284.4 73.9 %reduce-scatter.18.cloned.1.call-done = bf16[256,2048]{1,0:T(8,128)(2,1)} async-done(((bf16[2048,2048]{1,0:T(8,128)(2,1)}), bf16[256,2048]{1,0:T(8,128)(2,1)}) %reduce-scatter.18.cloned.1.call-update) | async-done | bytes 1048592 | tf_op jit(solution)/shard_map/reduce_scatter | solution.py:101
  1360.2 73.5 %reduce-scatter.12.cloned.1.call-done = bf16[256,2048]{1,0:T(8,128)(2,1)} async-done(((bf16[2048,2048]{1,0:T(8,128)(2,1)}), bf16[256,2048]{1,0:T(8,128)(2,1)}) %reduce-scatter.12.cloned.1.call-update) | async-done | bytes 1048592 | tf_op jit(solution)/shard_map/reduce_scatter | solution.py:101
  1443.9 44.9 %reduce-scatter.20.cloned.1.call-done = bf16[512,384]{1,0:T(8,128)(2,1)} async-done(((bf16[2048,384]{1,0:T(8,128)(2,1)}), bf16[512,384]{1,0:T(8,128)(2,1)}) %reduce-scatter.20.cloned.1.call-update) | async-done | bytes 393232 | tf_op jit(solution)/shard_map/reduce_scatter | solution.py:125
  1499.1 47.7 %all-gather.44.cloned.1.call-done = bf16[4096,512]{1,0:T(8,128)(2,1)} async-done(((bf16[1024,512]{1,0:T(8,128)(2,1)}), bf16[4096,512]{1,0:T(8,128)(2,1)}) %all-gather.44.cloned.1.call-update) | async-done | bytes 4194320 | tf_op jit(solution)/shard_map/all_gather | solution.py:317
  1553.6 48.1 %all-gather.40.cloned.1.call-done = bf16[512,4096]{1,0:T(8,128)(2,1)} async-done(((bf16[512,1024]{1,0:T(8,128)(2,1)}), bf16[512,4096]{1,0:T(8,128)(2,1)}) %all-gather.40.cloned.1.call-update) | async-done | bytes 4194320 | tf_op jit(solution)/shard_map/all_gather | solution.py:314
  1608.3 48.4 %all-gather.42.cloned.1.call-done = bf16[512,4096]{1,0:T(8,128)(2,1)} async-done(((bf16[512,1024]{1,0:T(8,128)(2,1)}), bf16[512,4096]{1,0:T(8,128)(2,1)}) %all-gather.42.cloned.1.call-update) | async-done | bytes 4194320 | tf_op jit(solution)/shard_map/all_gather | solution.py:314
  1719.5 38.9 %psum.7 = f32[2,2048]{1,0:T(2,128)S(1)} all-reduce(f32[2,2048]{1,0:T(2,128)S(1)} %pad_maximum_fusion.11), channel_id=1, replica_groups=mesh['dp'=4,'mx'=4,'my'=2] {'dp','mx','my'}, use_global_device_ids=true, to_apply=%region_20.21 | all-reduce | flops 4096 | bytes 32768 | tf_op jit(solution)/shard_map/psum | solution.py:333
  (350 shorter events, 487.0 us)
Async XLA Ops:
  9.7 53.8 %all-to-all-start = ((bf16[4,256,512]{2,1,0:T(8,128)(2,1)}), bf16[4,256,512]{2,1,0:T(8,128)(2,1)S(1)}, u32[]{:S(2)}, u32[]{:S(2)}) async-start(bf16[4,256,512]{2,1,0:T(8,128)(2,1)} %pad_maximum_fusion.5), calls=%async_computation | async-start | bytes 2097152 | tf_op jit(solution)/shard_map/all_to_all | solution.py:110
  17.2 106.5 %all-gather.18.cloned.1.call-start = ((), (), s32[]{:S(2)}) async-start(), calls=%async_computation.13 | async-start | bytes 9437184 | tf_op jit(solution)/shard_map/all_gather | solution.py:97
  67.7 111.2 %all-gather.22.cloned.1.call-start = ((), (), s32[]{:S(2)}) async-start(), calls=%async_computation.15 | async-start | bytes 2621440 | tf_op jit(solution)/shard_map/all_gather | solution.py:121
  132.6 109.4 %all-gather.24.cloned.1.call-start = ((), (), s32[]{:S(2)}) async-start(), calls=%async_computation.16 | async-start | bytes 1310720 | tf_op jit(solution)/shard_map/all_gather | solution.py:121
  134.3 184.9 %reduce-scatter.10.cloned.1.call-start = ((), (), s32[]{:S(2)}) async-start(), calls=%async_computation.17 | async-start | bytes 9437184 | tf_op jit(solution)/shard_map/reduce_scatter | solution.py:101
  249.4 242.6 %all-gather.28.cloned.1.call-start = ((), (), s32[]{:S(2)}) async-start(), calls=%async_computation.19 | async-start | bytes 10485760 | tf_op jit(solution)/shard_map/all_gather | solution.py:121
  252.7 294.1 %all-gather.26.cloned.1.call-start = ((), (), s32[]{:S(2)}) async-start(), calls=%async_computation.18 | async-start | bytes 9437184 | tf_op jit(solution)/shard_map/all_gather | solution.py:97
  322.5 307.3 %all-gather.30.cloned.1.call-start = ((), (), s32[]{:S(2)}) async-start(), calls=%async_computation.20 | async-start | bytes 5242880 | tf_op jit(solution)/shard_map/all_gather | solution.py:121
  324.8 360.2 %all-gather.32.cloned.1.call-start = ((), (), s32[]{:S(2)}) async-start(), calls=%async_computation.22 | async-start | bytes 9437184 | tf_op jit(solution)/shard_map/all_gather | solution.py:97
  387.6 415.3 %reduce-scatter.14.cloned.1.call-start = ((), (), s32[]{:S(2)}) async-start(), calls=%async_computation.23 | async-start | bytes 9437184 | tf_op jit(solution)/shard_map/reduce_scatter | solution.py:101
  731.2 130.8 %all-gather.34.cloned.1.call-start = ((), (), s32[]{:S(2)}) async-start(), calls=%async_computation.24 | async-start | bytes 9437184 | tf_op jit(solution)/shard_map/all_gather | solution.py:97
  807.6 227.7 %reduce-scatter.16.cloned.1.call-start = ((), (), s32[]{:S(2)}) async-start(), calls=%async_computation.25 | async-start | bytes 2621440 | tf_op jit(solution)/shard_map/reduce_scatter | solution.py:125
  984.3 122.1 %reduce-scatter.26.cloned.1.call-start = ((), (), s32[]{:S(2)}) async-start(), calls=%async_computation.34 | async-start | bytes 5242880 | tf_op jit(solution)/shard_map/reduce_scatter | solution.py:125
  998.2 256.1 %reduce-scatter.24.cloned.1.call-start = ((), (), s32[]{:S(2)}) async-start(), calls=%async_computation.31 | async-start | bytes 10485760 | tf_op jit(solution)/shard_map/reduce_scatter | solution.py:125
  1022.2 262.2 %reduce-scatter.22.cloned.1.call-start = ((), (), s32[]{:S(2)}) async-start(), calls=%async_computation.29 | async-start | bytes 1310720 | tf_op jit(solution)/shard_map/reduce_scatter | solution.py:125
  1032.1 326.2 %reduce-scatter.18.cloned.1.call-start = ((), (), s32[]{:S(2)}) async-start(), calls=%async_computation.26 | async-start | bytes 9437184 | tf_op jit(solution)/shard_map/reduce_scatter | solution.py:101
  1044.8 389.0 %reduce-scatter.12.cloned.1.call-start = ((), (), s32[]{:S(2)}) async-start(), calls=%async_computation.21 | async-start | bytes 9437184 | tf_op jit(solution)/shard_map/reduce_scatter | solution.py:101
  1059.1 429.7 %reduce-scatter.20.cloned.1.call-start = ((), (), s32[]{:S(2)}) async-start(), calls=%async_computation.27 | async-start | bytes 1966080 | tf_op jit(solution)/shard_map/reduce_scatter | solution.py:125
  1068.3 478.5 %all-gather.44.cloned.1.call-start = ((), (), s32[]{:S(2)}) async-start(), calls=%async_computation.35 | async-start | bytes 5242880 | tf_op jit(solution)/shard_map/all_gather | solution.py:317
  1106.4 495.2 %all-gather.40.cloned.1.call-start = ((), (), s32[]{:S(2)}) async-start(), calls=%async_computation.32 | async-start | bytes 5242880 | tf_op jit(solution)/shard_map/all_gather | solution.py:314
  1257.4 399.3 %all-gather.42.cloned.1.call-start = ((), (), s32[]{:S(2)}) async-start(), calls=%async_computation.33 | async-start | bytes 5242880 | tf_op jit(solution)/shard_map/all_gather | solution.py:314
  1258.1 426.9 %all-gather.38.cloned.1.call-start = ((), (), s32[]{:S(2)}) async-start(), calls=%async_computation.30 | async-start | bytes 1310720 | tf_op jit(solution)/shard_map/all_gather | solution.py:317
  1443.9 272.8 %all-gather.36.cloned.1.call-start = ((), (), s32[]{:S(2)}) async-start(), calls=%async_computation.28 | async-start | bytes 1310720 | tf_op jit(solution)/shard_map/all_gather | solution.py:314
  1493.0 266.0 %all-to-all-start.3 = ((bf16[256,4,512]{2,0,1:T(8,128)(2,1)}), bf16[256,4,512]{2,0,1:T(8,128)(2,1)S(1)}, u32[]{:S(2)}, u32[]{:S(2)}) async-start(bf16[256,4,512]{2,0,1:T(8,128)(2,1)} %bitcast.286), calls=%async_computation.8 | async-start | bytes 2097152 | tf_op jit(solution)/shard_map/all_to_all | solution.py:117
  (41 other events, 3936.7 us)
Sparse Core Ops, SparseCore 0:
  19.0 48.6 all-gather.19
  70.2 53.4 all-gather.17
  132.7 46.2 all-gather.21
  181.0 26.1 all-gather.23
  249.5 69.6 reduce-scatter.9
  321.2 170.6 all-gather.27
  494.4 52.3 all-gather.25
  548.9 80.7 all-gather.29
  632.2 52.7 all-gather.31
  731.3 71.4 reduce-scatter.13
  807.7 54.2 all-gather.33
  984.4 43.6 reduce-scatter.15
  1030.3 75.9 reduce-scatter.25
  1109.1 145.1 reduce-scatter.23
  1256.5 27.8 reduce-scatter.21
  1288.3 70.0 reduce-scatter.17
  1362.2 71.4 reduce-scatter.11
  1436.5 52.2 reduce-scatter.19
  1490.6 56.1 all-gather.43
  1549.0 52.5 all-gather.39
  1604.1 52.5 all-gather.41
  1658.5 26.4 all-gather.37
  1686.9 28.7 all-gather.35
